TPU v7x, 512 devices: a whole 4x8x8 slice. The times are simulated.
512 devices in a mesh: ctx: 16 (over z, core), head: 32 (over x, y).
Axes of the slice: x: 4, y: 8, z: 8, core: 2. Of those that a mesh axis runs over, the one named last changes fastest.
Arguments:
- x_in: bfloat16 [4096, 16384], P(('ctx', 'head')), may hold values from -6 to 6
- grad_y: bfloat16 [4096, 16384], P(('ctx', 'head')), may hold values from -6 to 6
- b_in: bfloat16 [4096, 2048], P(('ctx', 'head')), may hold values from -0.29882812 to 0.29882812
- c_in: bfloat16 [4096, 2048], P(('ctx', 'head')), may hold values from -0.375 to 0.375
- dt: bfloat16 [4096, 256], P(('ctx', 'head')), may hold values from 0.25 to 2
- conv_weight: float32 [4, 16384], P(None, 'head'), may hold values from -3 to 3
- conv_bias: float32 [16384], P('head'), may hold values from -3 to 3
- decay_rate: float32 [256], P('head'), may hold values from 1e-05 to 0.02
- skip: float32 [256], P('head'), may hold values from 0.5 to 1.5
Outputs:
- grad_x: bfloat16 [4096, 16384], P(('ctx', 'head'))
- grad_b: bfloat16 [4096, 2048], P(('ctx', 'head'))
- grad_c: bfloat16 [4096, 2048], P(('ctx', 'head'))
- grad_dt: float32 [4096, 256], P(('ctx', 'head'))
All inputs are finite; a program needn't handle non-finite values.
Results may differ from a plain program's by a relative error of at most 0.001.
Values may be sent and summed in bfloat16 or wider, within the bound.
A program may use at most 64 MiB of HBM per device.

v0:
```python
import math
import jax
import jax.numpy as jnp
from jax import lax
from jax.sharding import PartitionSpec as P

HEAD_DIM = 64
STATE = 256
GROUPS = 8
CONV = 4
HIGH = lax.Precision.HIGHEST


def passed_along(value, axis, by):
    count = lax.axis_size(axis)
    pairs = [(i, i + by) for i in range(count) if 0 <= i + by < count]
    return lax.ppermute(value, axis, pairs)


def entering(value, axis, combine, identity, reverse):
    count, place = (lax.axis_size(axis), lax.axis_index(axis))
    everything = jax.tree.map(lambda part: lax.all_gather(part, axis), value)
    start = jax.tree.map(
        lambda part, zero: jnp.broadcast_to(jnp.asarray(zero, part.dtype), part.shape),
        value,
        identity,
    )

    def hop(k, before):
        at = count - 1 - k if reverse else k
        reached = at > place if reverse else at < place
        new = combine(before, jax.tree.map(lambda part: part[at], everything))
        return jax.tree.map(lambda a, b: jnp.where(reached, a, b), new, before)

    return lax.fori_loop(0, count, hop, start)


def conv_silu(padded, weight, bias):
    length = padded.shape[0] - CONV + 1
    summed = bias[None, :] + weight[0][None, :] * padded[0:length]
    for k in range(1, CONV):
        summed = summed + weight[k][None, :] * padded[k : k + length]
    return jax.nn.silu(summed)


def head_forward(
    ext_rows, dt_head, gram_blocks, b_rows, c_rows, weight, bias, head_rate, skip_head, state_in
):
    activ = conv_silu(ext_rows, weight, bias)
    length = activ.shape[0]
    width = gram_blocks.shape[1]
    count = length // width
    causal = lax.broadcasted_iota(jnp.int32, (width, width), 0) >= lax.broadcasted_iota(
        jnp.int32, (width, width), 1
    )
    pieces = (
        activ.reshape(count, width, HEAD_DIM),
        dt_head.reshape(count, width),
        gram_blocks,
        b_rows.reshape(count, width, STATE),
        c_rows.reshape(count, width, STATE),
    )

    def advance(carried, piece):
        act_part, dt_part, gram_part, b_part, c_part = piece
        cumul = jnp.cumsum(-dt_part * head_rate)
        gaps = cumul[:, None] - cumul[None, :]
        decay_mat = jnp.where(causal, jnp.exp(jnp.where(causal, gaps, 0.0)), 0.0)
        mixing = decay_mat * gram_part * dt_part[None, :]
        output = jnp.dot(mixing, act_part, precision=HIGH)
        output = output + jnp.exp(cumul)[:, None] * jnp.dot(c_part, carried.T, precision=HIGH)
        tail_wt = jnp.exp(cumul[-1] - cumul) * dt_part
        carried = jnp.exp(cumul[-1]) * carried + jnp.dot(
            (act_part * tail_wt[:, None]).T, b_part, precision=HIGH
        )
        return (carried, output)

    state_out, outputs = lax.scan(advance, state_in, pieces)
    output = outputs.reshape(length, HEAD_DIM) + skip_head * activ
    return (output, state_out)


def forward_combine(earlier, later):
    return (earlier[0] * later[0], later[0][:, None, None] * earlier[1] + later[1])


def backward_combine(earlier, later):
    return (earlier[0] * later[0], later[1] + later[0][:, None, None] * earlier[1])


def shards(x_in, grad_y, b_in, c_in, dt, conv_weight, conv_bias, decay_rate, skip):
    n_head = lax.axis_size("head")
    per_group = n_head // GROUPS
    tok_dev = x_in.shape[0]
    heads_dev = decay_rate.shape[0]
    x_rows, dy_rows, dt_rows = (
        lax.all_to_all(x_in, "head", split_axis=1, concat_axis=0, tiled=True),
        lax.all_to_all(grad_y, "head", split_axis=1, concat_axis=0, tiled=True),
        lax.all_to_all(dt, "head", split_axis=1, concat_axis=0, tiled=True),
    )
    b_all, c_all = (
        lax.all_gather(b_in, "head", axis=0, tiled=True),
        lax.all_gather(c_in, "head", axis=0, tiled=True),
    )
    first = lax.axis_index("head") // per_group * STATE
    b_rows = lax.dynamic_slice_in_dim(b_all, first, STATE, 1)
    c_rows = lax.dynamic_slice_in_dim(c_all, first, STATE, 1)
    length = x_rows.shape[0]
    width = math.gcd(length, 128)
    count = length // width
    edge = passed_along(x_rows[length - CONV + 1 :], "ctx", 1)
    ext_rows = jnp.concatenate([edge, x_rows], axis=0).astype(jnp.float32)
    b_mat = b_rows.astype(jnp.float32)
    c_mat = c_rows.astype(jnp.float32)
    dt_mat = dt_rows.astype(jnp.float32)
    dy_mat = dy_rows.astype(jnp.float32).reshape(length, heads_dev, HEAD_DIM)
    activ = conv_silu(ext_rows, conv_weight, conv_bias).reshape(length, heads_dev, HEAD_DIM)
    cumul = jnp.cumsum(-dt_mat * decay_rate[None, :], axis=0)
    block_decay = jnp.exp(cumul[-1])
    tail_wt = jnp.exp(cumul[-1][None, :] - cumul) * dt_mat
    local_state = jnp.einsum("shp,sn->hpn", activ * tail_wt[:, :, None], b_mat, precision=HIGH)
    local_pull = jnp.einsum(
        "shp,sn->hpn", dy_mat * jnp.exp(cumul)[:, :, None], c_mat, precision=HIGH
    )
    identity = (
        jnp.ones((heads_dev,), jnp.float32),
        jnp.zeros((heads_dev, HEAD_DIM, STATE), jnp.float32),
    )
    _, state_in = entering((block_decay, local_state), "ctx", forward_combine, identity, False)
    _, state_grad = entering((block_decay, local_pull), "ctx", backward_combine, identity, True)
    b_blocks = b_mat.reshape(count, width, STATE)
    c_blocks = c_mat.reshape(count, width, STATE)
    gram_blocks = jnp.einsum("cwn,cvn->cwv", c_blocks, b_blocks, precision=HIGH)

    def head_step(sums, pieces):
        ext_head, dt_head, weight, bias, head_rate, skip_head, head_state, dy_head, head_grad = (
            pieces
        )

        def forward_fn(ext_arg, dt_arg, gram_arg, b_arg, c_arg):
            return head_forward(
                ext_arg,
                dt_arg,
                gram_arg,
                b_arg,
                c_arg,
                weight,
                bias,
                head_rate,
                skip_head,
                head_state,
            )

        _, pullback = jax.vjp(forward_fn, ext_head, dt_head, gram_blocks, b_mat, c_mat)
        g_ext, g_dt, g_gram, g_b, g_c = pullback((dy_head, head_grad))
        return ((sums[0] + g_gram, sums[1] + g_b, sums[2] + g_c), (g_ext, g_dt))

    ext_heads = ext_rows.reshape(length + CONV - 1, heads_dev, HEAD_DIM).transpose(1, 0, 2)
    weight_heads = conv_weight.reshape(CONV, heads_dev, HEAD_DIM).transpose(1, 0, 2)
    bias_heads = conv_bias.reshape(heads_dev, HEAD_DIM)
    start = (
        jnp.zeros((count, width, width), jnp.float32),
        jnp.zeros((length, STATE), jnp.float32),
        jnp.zeros((length, STATE), jnp.float32),
    )
    inputs = (
        ext_heads,
        dt_mat.T,
        weight_heads,
        bias_heads,
        decay_rate,
        skip,
        state_in,
        dy_mat.transpose(1, 0, 2),
        state_grad,
    )
    sums, per_head = lax.scan(head_step, start, inputs)
    g_gram, g_b, g_c = sums
    g_b = g_b + jnp.einsum("cwv,cwn->cvn", g_gram, c_blocks, precision=HIGH).reshape(length, STATE)
    g_c = g_c + jnp.einsum("cwv,cvn->cwn", g_gram, b_blocks, precision=HIGH).reshape(length, STATE)
    g_ext = per_head[0].transpose(1, 0, 2).reshape(length + CONV - 1, heads_dev * HEAD_DIM)
    g_dt = per_head[1].T
    carried_back = passed_along(g_ext[: CONV - 1], "ctx", -1)
    g_local = g_ext[CONV - 1 :]
    g_local = g_local.at[length - CONV + 1 :].add(carried_back)
    grad_x = lax.all_to_all(
        g_local.astype(jnp.bfloat16), "head", split_axis=0, concat_axis=1, tiled=True
    )
    grad_dt, b_parts, c_parts = (
        lax.all_to_all(g_dt, "head", split_axis=0, concat_axis=1, tiled=True),
        lax.all_to_all(g_b, "head", split_axis=0, concat_axis=1, tiled=True),
        lax.all_to_all(g_c, "head", split_axis=0, concat_axis=1, tiled=True),
    )
    grad_b = (
        b_parts.reshape(tok_dev, GROUPS, per_group, STATE)
        .sum(axis=2)
        .reshape(tok_dev, GROUPS * STATE)
    )
    grad_c = (
        c_parts.reshape(tok_dev, GROUPS, per_group, STATE)
        .sum(axis=2)
        .reshape(tok_dev, GROUPS * STATE)
    )
    return (grad_x, grad_b.astype(jnp.bfloat16), grad_c.astype(jnp.bfloat16), grad_dt)


def solution(mesh):
    in_specs = (
        P(("ctx", "head"), None),
        P(("ctx", "head"), None),
        P(("ctx", "head"), None),
        P(("ctx", "head"), None),
        P(("ctx", "head"), None),
        P(None, "head"),
        P("head"),
        P("head"),
        P("head"),
    )
    out_specs = (
        P(("ctx", "head"), None),
        P(("ctx", "head"), None),
        P(("ctx", "head"), None),
        P(("ctx", "head"), None),
    )
    return jax.shard_map(shards, mesh=mesh, in_specs=in_specs, out_specs=out_specs, check_vma=False)
```

profile of v0, /device:TPU:1, one launch (start us, length us, event | category | flops | bytes accessed | tf_op | source)
XLA Modules:
  0.0 932.1 jit_solution(3826005962519937768)
XLA Ops:
  10.1 10.5 %all-to-all-start.1 = ((bf16[8,32,8]{2,0,1:T(8,128)(2,1)}), bf16[8,32,8]{2,0,1:T(8,128)(2,1)S(1)}, u32[]{:S(2)}, u32[]{:S(2)}) async-start(bf16[8,32,8]{2,0,1:T(8,128)(2,1)} %copy.117), calls=%async_computation.1 | async-start | bytes 131072 | tf_op jit(solution)/shard_map/all_to_all | solution.py:99
  20.7 8.8 all-to-all-done.1
  29.5 3.9 all-to-all-start
  35.9 7.2 all-to-all-done
  45.9 48.0 %all-gather.8.cloned.1.call-done = bf16[256,2048]{1,0:T(8,128)(2,1)} async-done(((bf16[8,2048]{1,0:T(8,128)(2,1)}), bf16[256,2048]{1,0:T(8,128)(2,1)}) %all-gather.8.cloned.1.call-update) | async-done | bytes 1048592 | tf_op jit(solution)/shard_map/all_gather | solution.py:103
  96.7 5.7 all-to-all-start.2
  102.6 9.4 %all-to-all-done.2 = bf16[8,32,512]{2,0,1:T(8,128)(2,1)S(1)} async-done(((bf16[8,32,512]{2,0,1:T(8,128)(2,1)}), bf16[8,32,512]{2,0,1:T(8,128)(2,1)S(1)}, u32[]{:S(2)}, u32[]{:S(2)}) %all-to-all-start.2) | async-done | bytes 262176 | tf_op jit(solution)/shard_map/all_to_all | solution.py:97
  112.0 9.9 %collective-permute-start = (bf16[3,512]{1,0:T(4,128)(2,1)S(1)}, bf16[3,512]{1,0:T(4,128)(2,1)S(1)}, u32[]{:S(2)}, u32[]{:S(2)}) collective-permute-start(bf16[3,512]{1,0:T(4,128)(2,1)S(1)} %slice.212), channel_id=1, source_target_pairs={{0,32},{32,64},{64,96},{96,128},{128,160},{160,192},{192,224},{224... | collective-permute-start | bytes 9224 | tf_op jit(solution)/shard_map/ppermute | solution.py:17
  123.4 53.1 %all-gather.10.cloned.1.call-done = bf16[256,2048]{1,0:T(8,128)(2,1)} async-done(((bf16[8,2048]{1,0:T(8,128)(2,1)}), bf16[256,2048]{1,0:T(8,128)(2,1)}) %all-gather.10.cloned.1.call-update) | async-done | bytes 1048592 | tf_op jit(solution)/shard_map/all_gather | solution.py:102
  180.1 22.8 %all-gather.2 = f32[16,1,8]{2,1,0:T(1,128)S(1)} all-gather(f32[1,1,8]{2,1,0:T(1,128)S(1)} %bitcast.532), channel_id=1, replica_groups=mesh['ctx'=16,'head'=32] {'ctx'}, dimensions={0}, use_global_device_ids=true | all-gather | bytes 544 | tf_op jit(solution)/shard_map/all_gather | solution.py:22
  204.4 36.4 %all-gather.12.cloned.1.call-done = f32[128,64,256]{2,1,0:T(8,128)} async-done(((f32[8,64,256]{2,1,0:T(8,128)}), f32[128,64,256]{2,1,0:T(8,128)}) %all-gather.12.cloned.1.call-update) | async-done | bytes 8388624 | tf_op jit(solution)/shard_map/all_gather | solution.py:22
  240.8 34.0 %while.180 = (s32[]{:T(128)}, f32[8,64,256]{2,1,0:T(8,128)}, s32[]{:T(128)}, f32[16,8,64,256]{3,2,1,0:T(8,128)}, f32[16,8]{1,0:T(8,128)S(1)}, /*index=5*/s32[]{:T(128)}, s32[]{:T(128)}, s32[]{:T(128)}, s32[]{:T(128)}) while((s32[]{:T(128)}, f32[8,64,256]{2,1,0:T(8,128)}, s32[]{:T(128)}, f32[16,8,64,256]{3,2,1,0:T(8,128)}, ...), condition=%wide.region_5.6_spmd.clone, body=%wide.region_4.5_spmd.clone.sunk | while | flops 524296 | bytes 1573127 | solution.py:35
  240.8 2.0 fusion.141
  242.8 2.1 fusion.141
  244.9 2.1 fusion.141
  247.0 2.1 fusion.141
  249.2 2.1 fusion.141
  251.3 2.1 fusion.141
  253.4 2.1 fusion.141
  255.5 2.1 fusion.141
  257.6 2.1 fusion.141
  259.8 2.1 fusion.141
  261.9 2.2 fusion.141
  264.1 2.1 fusion.141
  266.2 2.2 fusion.141
  268.4 2.1 fusion.141
  270.5 2.2 fusion.141
  272.7 2.1 fusion.141
  274.8 25.4 %all-gather.14.cloned.1.call-done = f32[128,64,256]{2,1,0:T(8,128)} async-done(((f32[8,64,256]{2,1,0:T(8,128)}), f32[128,64,256]{2,1,0:T(8,128)}) %all-gather.14.cloned.1.call-update) | async-done | bytes 8388624 | tf_op jit(solution)/shard_map/all_gather | solution.py:22
  300.2 19.4 %while.181 = (s32[]{:T(128)}, f32[8,64,256]{2,1,0:T(8,128)S(1)}, s32[]{:T(128)}, f32[16,8]{1,0:T(8,128)S(1)}, f32[16,8,64,256]{3,2,1,0:T(8,128)}, /*index=5*/s32[]{:T(128)}, s32[]{:T(128)}) while((s32[]{:T(128)}, f32[8,64,256]{2,1,0:T(8,128)S(1)}, s32[]{:T(128)}, f32[16,8]{1,0:T(8,128)S(1)}, f32[16,8,64,256]{3,2,1,0:T(8,128)}, ...), condition=%wide.region_3.4_spmd.clone, body=%wide.region_2.3_spmd.clone.sunk | while | flops 524292 | bytes 1573065 | solution.py:35
  319.6 532.5 %while.184 = (s32[]{:T(128)}, f32[2,128,128]{2,1,0:T(8,128)}, f32[256,256]{1,0:T(8,128)}, f32[256,256]{1,0:T(8,128)}, f32[8,259,64]{1,2,0:T(8,128)}, /*index=5*/...) while((s32[]{:T(128)}, f32[2,128,128]{2,1,0:T(8,128)}, ...), condition=%wide.region_20.21_spmd.clone, body=%wide.region_6.20_spmd.clone.sunk | while | flops 177621440 | bytes 10403926 | solution.py:177
  320.4 2.9 constant_dynamic-slice_fusion.26
  327.2 12.2 %while.185 = (s32[]{:T(128)}, f32[64,256]{1,0:T(8,128)S(1)}, f32[2,128,128]{2,1,0:T(8,128)S(1)}, f32[2,128,128]{2,1,0:T(8,128)S(1)}, f32[2,1,128]{2,1,0:T(1,128)...) while((s32[]{:T(128)}, f32[64,256]{1,0:T(8,128)S(1)}, ...), condition=%wide.region_9.9_spmd.clone.clone, body=%wide.region_7.8_spmd.clone.clone.sunk | while | flops 50496128 | bytes 1198381 | solution.py:78
  343.5 32.7 %while.186 = (s32[]{:T(128)}, f32[64,256]{1,0:T(8,128)S(1)}, f32[2,128,64]{1,2,0:T(8,128)}, f32[2,128]{1,0:T(2,128)}, f32[2,128,128]{2,1,0:T(8,128)}, /*index=5*...) while((s32[]{:T(128)}, f32[64,256]{1,0:T(8,128)S(1)}, ...), condition=%wide.region_19.19_spmd.clone.clone, body=%wide.region_10.18_spmd.clone.clone.sunk | while | flops 126174464 | bytes 2319733 | solution.py:78
  386.0 2.9 constant_dynamic-slice_fusion.26
  392.8 12.2 %while.185 = (s32[]{:T(128)}, f32[64,256]{1,0:T(8,128)S(1)}, f32[2,128,128]{2,1,0:T(8,128)S(1)}, f32[2,128,128]{2,1,0:T(8,128)S(1)}, f32[2,1,128]{2,1,0:T(1,128)...) while((s32[]{:T(128)}, f32[64,256]{1,0:T(8,128)S(1)}, ...), condition=%wide.region_9.9_spmd.clone.clone, body=%wide.region_7.8_spmd.clone.clone.sunk | while | flops 50496128 | bytes 1198381 | solution.py:78
  409.1 32.7 %while.186 = (s32[]{:T(128)}, f32[64,256]{1,0:T(8,128)S(1)}, f32[2,128,64]{1,2,0:T(8,128)}, f32[2,128]{1,0:T(2,128)}, f32[2,128,128]{2,1,0:T(8,128)}, /*index=5*...) while((s32[]{:T(128)}, f32[64,256]{1,0:T(8,128)S(1)}, ...), condition=%wide.region_19.19_spmd.clone.clone, body=%wide.region_10.18_spmd.clone.clone.sunk | while | flops 126174464 | bytes 2319733 | solution.py:78
  452.7 2.9 constant_dynamic-slice_fusion.26
  459.5 12.2 %while.185 = (s32[]{:T(128)}, f32[64,256]{1,0:T(8,128)S(1)}, f32[2,128,128]{2,1,0:T(8,128)S(1)}, f32[2,128,128]{2,1,0:T(8,128)S(1)}, f32[2,1,128]{2,1,0:T(1,128)...) while((s32[]{:T(128)}, f32[64,256]{1,0:T(8,128)S(1)}, ...), condition=%wide.region_9.9_spmd.clone.clone, body=%wide.region_7.8_spmd.clone.clone.sunk | while | flops 50496128 | bytes 1198381 | solution.py:78
  475.8 32.7 %while.186 = (s32[]{:T(128)}, f32[64,256]{1,0:T(8,128)S(1)}, f32[2,128,64]{1,2,0:T(8,128)}, f32[2,128]{1,0:T(2,128)}, f32[2,128,128]{2,1,0:T(8,128)}, /*index=5*...) while((s32[]{:T(128)}, f32[64,256]{1,0:T(8,128)S(1)}, ...), condition=%wide.region_19.19_spmd.clone.clone, body=%wide.region_10.18_spmd.clone.clone.sunk | while | flops 126174464 | bytes 2319733 | solution.py:78
  519.4 2.9 constant_dynamic-slice_fusion.26
  526.2 12.2 %while.185 = (s32[]{:T(128)}, f32[64,256]{1,0:T(8,128)S(1)}, f32[2,128,128]{2,1,0:T(8,128)S(1)}, f32[2,128,128]{2,1,0:T(8,128)S(1)}, f32[2,1,128]{2,1,0:T(1,128)...) while((s32[]{:T(128)}, f32[64,256]{1,0:T(8,128)S(1)}, ...), condition=%wide.region_9.9_spmd.clone.clone, body=%wide.region_7.8_spmd.clone.clone.sunk | while | flops 50496128 | bytes 1198381 | solution.py:78
  542.5 32.7 %while.186 = (s32[]{:T(128)}, f32[64,256]{1,0:T(8,128)S(1)}, f32[2,128,64]{1,2,0:T(8,128)}, f32[2,128]{1,0:T(2,128)}, f32[2,128,128]{2,1,0:T(8,128)}, /*index=5*...) while((s32[]{:T(128)}, f32[64,256]{1,0:T(8,128)S(1)}, ...), condition=%wide.region_19.19_spmd.clone.clone, body=%wide.region_10.18_spmd.clone.clone.sunk | while | flops 126174464 | bytes 2319733 | solution.py:78
  586.1 2.9 constant_dynamic-slice_fusion.26
  592.9 12.2 %while.185 = (s32[]{:T(128)}, f32[64,256]{1,0:T(8,128)S(1)}, f32[2,128,128]{2,1,0:T(8,128)S(1)}, f32[2,128,128]{2,1,0:T(8,128)S(1)}, f32[2,1,128]{2,1,0:T(1,128)...) while((s32[]{:T(128)}, f32[64,256]{1,0:T(8,128)S(1)}, ...), condition=%wide.region_9.9_spmd.clone.clone, body=%wide.region_7.8_spmd.clone.clone.sunk | while | flops 50496128 | bytes 1198381 | solution.py:78
  609.2 32.7 %while.186 = (s32[]{:T(128)}, f32[64,256]{1,0:T(8,128)S(1)}, f32[2,128,64]{1,2,0:T(8,128)}, f32[2,128]{1,0:T(2,128)}, f32[2,128,128]{2,1,0:T(8,128)}, /*index=5*...) while((s32[]{:T(128)}, f32[64,256]{1,0:T(8,128)S(1)}, ...), condition=%wide.region_19.19_spmd.clone.clone, body=%wide.region_10.18_spmd.clone.clone.sunk | while | flops 126174464 | bytes 2319733 | solution.py:78
  652.8 2.9 constant_dynamic-slice_fusion.26
  659.5 12.2 %while.185 = (s32[]{:T(128)}, f32[64,256]{1,0:T(8,128)S(1)}, f32[2,128,128]{2,1,0:T(8,128)S(1)}, f32[2,128,128]{2,1,0:T(8,128)S(1)}, f32[2,1,128]{2,1,0:T(1,128)...) while((s32[]{:T(128)}, f32[64,256]{1,0:T(8,128)S(1)}, ...), condition=%wide.region_9.9_spmd.clone.clone, body=%wide.region_7.8_spmd.clone.clone.sunk | while | flops 50496128 | bytes 1198381 | solution.py:78
  675.9 32.7 %while.186 = (s32[]{:T(128)}, f32[64,256]{1,0:T(8,128)S(1)}, f32[2,128,64]{1,2,0:T(8,128)}, f32[2,128]{1,0:T(2,128)}, f32[2,128,128]{2,1,0:T(8,128)}, /*index=5*...) while((s32[]{:T(128)}, f32[64,256]{1,0:T(8,128)S(1)}, ...), condition=%wide.region_19.19_spmd.clone.clone, body=%wide.region_10.18_spmd.clone.clone.sunk | while | flops 126174464 | bytes 2319733 | solution.py:78
  719.5 2.9 constant_dynamic-slice_fusion.26
  726.2 12.2 %while.185 = (s32[]{:T(128)}, f32[64,256]{1,0:T(8,128)S(1)}, f32[2,128,128]{2,1,0:T(8,128)S(1)}, f32[2,128,128]{2,1,0:T(8,128)S(1)}, f32[2,1,128]{2,1,0:T(1,128)...) while((s32[]{:T(128)}, f32[64,256]{1,0:T(8,128)S(1)}, ...), condition=%wide.region_9.9_spmd.clone.clone, body=%wide.region_7.8_spmd.clone.clone.sunk | while | flops 50496128 | bytes 1198381 | solution.py:78
  742.6 32.7 %while.186 = (s32[]{:T(128)}, f32[64,256]{1,0:T(8,128)S(1)}, f32[2,128,64]{1,2,0:T(8,128)}, f32[2,128]{1,0:T(2,128)}, f32[2,128,128]{2,1,0:T(8,128)}, /*index=5*...) while((s32[]{:T(128)}, f32[64,256]{1,0:T(8,128)S(1)}, ...), condition=%wide.region_19.19_spmd.clone.clone, body=%wide.region_10.18_spmd.clone.clone.sunk | while | flops 126174464 | bytes 2319733 | solution.py:78
  786.1 2.9 constant_dynamic-slice_fusion.26
  792.9 12.2 %while.185 = (s32[]{:T(128)}, f32[64,256]{1,0:T(8,128)S(1)}, f32[2,128,128]{2,1,0:T(8,128)S(1)}, f32[2,128,128]{2,1,0:T(8,128)S(1)}, f32[2,1,128]{2,1,0:T(1,128)...) while((s32[]{:T(128)}, f32[64,256]{1,0:T(8,128)S(1)}, ...), condition=%wide.region_9.9_spmd.clone.clone, body=%wide.region_7.8_spmd.clone.clone.sunk | while | flops 50496128 | bytes 1198381 | solution.py:78
  809.3 32.7 %while.186 = (s32[]{:T(128)}, f32[64,256]{1,0:T(8,128)S(1)}, f32[2,128,64]{1,2,0:T(8,128)}, f32[2,128]{1,0:T(2,128)}, f32[2,128,128]{2,1,0:T(8,128)}, /*index=5*...) while((s32[]{:T(128)}, f32[64,256]{1,0:T(8,128)S(1)}, ...), condition=%wide.region_19.19_spmd.clone.clone, body=%wide.region_10.18_spmd.clone.clone.sunk | while | flops 126174464 | bytes 2319733 | solution.py:78
  854.8 9.3 all-to-all-start.6
  865.8 7.5 all-to-all-done.6
  873.2 4.6 all-to-all-start.5
  880.8 6.7 all-to-all-done.5
  887.5 6.3 all-to-all-start.4
  894.8 3.8 collective-permute-start.1
  899.9 2.9 collective-permute-done.1
  904.5 8.9 all-to-all-start.3
  915.4 9.4 %all-to-all-done.3 = bf16[32,8,512]{2,1,0:T(8,128)(2,1)S(1)} async-done(((bf16[32,8,512]{2,1,0:T(8,128)(2,1)}), bf16[32,8,512]{2,1,0:T(8,128)(2,1)S(1)}, u32[]{:S(2)}, u32[]{:S(2)}) %all-to-all-start.3) | async-done | bytes 262176 | tf_op jit(solution)/shard_map/all_to_all | solution.py:186
  (1207 shorter events, 527.4 us)
Async XLA Ops:
  7.2 95.2 %copy-start.11 = (f32[4,512]{1,0:T(4,128)S(1)}, f32[4,512]{1,0:T(4,128)}, u32[]{:S(2)}) copy-start(f32[4,512]{1,0:T(4,128)} %param.26) | copy-start | bytes 24580
  7.2 115.6 %copy-start.12 = (f32[512]{0:T(512)S(1)}, f32[512]{0:T(512)}, u32[]{:S(2)}) copy-start(f32[512]{0:T(512)} %param.27) | copy-start | bytes 6148
  7.2 86.7 %all-gather.8.cloned.1.call-start = ((), (), s32[]{:S(2)}) async-start(), calls=%async_computation.7 | async-start | bytes 1081344 | tf_op jit(solution)/shard_map/all_gather | solution.py:103
  7.9 168.6 %all-gather.10.cloned.1.call-start = ((), (), s32[]{:S(2)}) async-start(), calls=%async_computation.8 | async-start | bytes 1081344 | tf_op jit(solution)/shard_map/all_gather | solution.py:102
  10.1 19.4 %all-to-all-start.1 = ((bf16[8,32,8]{2,0,1:T(8,128)(2,1)}), bf16[8,32,8]{2,0,1:T(8,128)(2,1)S(1)}, u32[]{:S(2)}, u32[]{:S(2)}) async-start(bf16[8,32,8]{2,0,1:T(8,128)(2,1)} %copy.117), calls=%async_computation.1 | async-start | bytes 131072 | tf_op jit(solution)/shard_map/all_to_all | solution.py:99
  29.5 13.5 %all-to-all-start = ((bf16[8,32,512]{2,0,1:T(8,128)(2,1)}), bf16[8,32,512]{2,0,1:T(8,128)(2,1)S(1)}, u32[]{:S(2)}, u32[]{:S(2)}) async-start(bf16[8,32,512]{2,0,1:T(8,128)(2,1)} %bitcast.520), calls=%async_computation | async-start | bytes 524288 | tf_op jit(solution)/shard_map/all_to_all | solution.py:98
  33.4 207.4 %all-gather.12.cloned.1.call-start = ((), (), s32[]{:S(2)}) async-start(), calls=%async_computation.9 | async-start | bytes 8912896 | tf_op jit(solution)/shard_map/all_gather | solution.py:22
  94.8 146.0 %copy-start.2 = (bf16[256,256]{1,0:T(8,128)(2,1)}, bf16[256,256]{1,0:T(8,128)(2,1)S(1)}, u32[]{:S(2)}) copy-start(bf16[256,256]{1,0:T(8,128)(2,1)S(1)} %get-tuple-element.2368) | copy-start | bytes 393220
  96.7 15.4 %all-to-all-start.2 = ((bf16[8,32,512]{2,0,1:T(8,128)(2,1)}), bf16[8,32,512]{2,0,1:T(8,128)(2,1)S(1)}, u32[]{:S(2)}, u32[]{:S(2)}) async-start(bf16[8,32,512]{2,0,1:T(8,128)(2,1)} %bitcast.16), calls=%async_computation.2 | async-start | bytes 524288 | tf_op jit(solution)/shard_map/all_to_all | solution.py:97
  102.4 197.9 %all-gather.14.cloned.1.call-start = ((), (), s32[]{:S(2)}) async-start(), calls=%async_computation.10 | async-start | bytes 8912896 | tf_op jit(solution)/shard_map/all_gather | solution.py:22
  112.0 10.7 %collective-permute-start = (bf16[3,512]{1,0:T(4,128)(2,1)S(1)}, bf16[3,512]{1,0:T(4,128)(2,1)S(1)}, u32[]{:S(2)}, u32[]{:S(2)}) collective-permute-start(bf16[3,512]{1,0:T(4,128)(2,1)S(1)} %slice.212), channel_id=1, source_target_pairs={{0,32},{32,64},{64,96},{96,128},{128,160},{160,192},{192,224},{224... | collective-permute-start | bytes 9224 | tf_op jit(solution)/shard_map/ppermute | solution.py:17
  177.4 122.8 %copy-start.1 = (bf16[256,256]{1,0:T(8,128)(2,1)}, bf16[256,256]{1,0:T(8,128)(2,1)S(1)}, u32[]{:S(2)}) copy-start(bf16[256,256]{1,0:T(8,128)(2,1)S(1)} %get-tuple-element.2370) | copy-start | bytes 393220
  320.4 6.2 copy-start.3
  320.4 6.2 copy-start.4
  320.4 6.2 copy-start.5
  320.4 6.2 copy-start.9
  339.4 2.2 copy-start.8
  339.4 2.2 copy-start.13
  386.0 6.2 copy-start.3
  386.0 6.2 copy-start.4
  386.0 6.2 copy-start.5
  386.0 6.2 copy-start.9
  405.0 2.2 copy-start.8
  405.0 2.2 copy-start.13
  452.7 6.2 copy-start.3
  452.7 6.2 copy-start.4
  452.7 6.2 copy-start.5
  452.7 6.2 copy-start.9
  471.7 2.2 copy-start.8
  471.7 2.2 copy-start.13
  519.4 6.2 copy-start.3
  519.4 6.2 copy-start.4
  519.4 6.2 copy-start.5
  519.4 6.2 copy-start.9
  538.4 2.2 copy-start.8
  538.4 2.2 copy-start.13
  586.0 6.2 copy-start.3
  586.0 6.2 copy-start.4
  586.0 6.2 copy-start.5
  586.1 6.2 copy-start.9
  605.0 2.2 copy-start.8
  605.0 2.2 copy-start.13
  652.7 6.2 copy-start.3
  652.7 6.2 copy-start.4
  652.7 6.2 copy-start.5
  652.8 6.2 copy-start.9
  671.7 2.2 copy-start.8
  671.7 2.2 copy-start.13
  719.4 6.2 copy-start.3
  719.4 6.2 copy-start.4
  719.4 6.2 copy-start.5
  719.5 6.2 copy-start.9
  738.4 2.2 copy-start.8
  738.4 2.2 copy-start.13
  786.1 6.2 copy-start.3
  786.1 6.2 copy-start.4
  786.1 6.2 copy-start.5
  786.1 6.2 copy-start.9
  805.1 2.2 copy-start.13
  854.8 18.4 %all-to-all-start.6 = ((f32[32,8,8]{1,2,0:T(8,128)}), f32[32,8,8]{1,2,0:T(8,128)S(1)}, u32[]{:S(2)}, u32[]{:S(2)}) async-start(f32[32,8,8]{1,2,0:T(8,128)} %copy.135), calls=%async_computation.6 | async-start | bytes 262144 | tf_op jit(solution)/shard_map/all_to_all | solution.py:190
  873.2 14.3 %all-to-all-start.5 = ((f32[32,8,256]{2,1,0:T(8,128)}), f32[32,8,256]{2,1,0:T(8,128)S(1)}, u32[]{:S(2)}, u32[]{:S(2)}) async-start(f32[32,8,256]{2,1,0:T(8,128)} %bitcast.44), calls=%async_computation.5 | async-start | bytes 524288 | tf_op jit(solution)/shard_map/all_to_all | solution.py:192
  887.5 17.0 %all-to-all-start.4 = ((f32[32,8,256]{2,1,0:T(8,128)}), f32[32,8,256]{2,1,0:T(8,128)S(1)}, u32[]{:S(2)}, u32[]{:S(2)}) async-start(f32[32,8,256]{2,1,0:T(8,128)} %bitcast.39), calls=%async_computation.4 | async-start | bytes 524288 | tf_op jit(solution)/shard_map/all_to_all | solution.py:191
  894.8 8.0 collective-permute-start.1
  904.5 20.3 %all-to-all-start.3 = ((bf16[32,8,512]{2,1,0:T(8,128)(2,1)}), bf16[32,8,512]{2,1,0:T(8,128)(2,1)S(1)}, u32[]{:S(2)}, u32[]{:S(2)}) async-start(bf16[32,8,512]{2,1,0:T(8,128)(2,1)} %bitcast.35), calls=%async_computation.3 | async-start | bytes 524288 | tf_op jit(solution)/shard_map/all_to_all | solution.py:186
  (33 other events, 72.9 us)
Sparse Core Ops, SparseCore 0:
  11.2 82.6 all-gather.7
  97.1 79.3 all-gather.9
  178.6 62.1 all-gather.11
  242.8 57.3 all-gather.13
where the time goes:
time: 941 us; the launch traced here: 932 us
  other arithmetic  270 us (29%)
  local copies, waits for them, and re-layouts  240 us (26%)
  waiting for transfers between devices  216 us (23%)
  matrix products  72.4 us (8%)
  starting transfers between devices  63 us (7%)
  loops' own time  33.3 us (4%)
  blocking collectives  22.8 us (2%)
  between operations  14.1 us (1%)
    all_gather x2, waiting for transfers between devices, entering(): everything = jax.tree.map(lambda part: lax.all_gather(part, axis), value)  61.8 us
    all_gather x1, waiting for transfers between devices, shards(): lax.all_gather(b_in, 'head', axis=0, tiled=True)  53.1 us
    select_n x32, other arithmetic, hop(): return jax.tree.map(lambda a, b: jnp.where(reached, a, b), new, before)  52.6 us
    dynamic_update_slice x112, local copies, waits for them, and re-layouts, head_forward(): state_out, outputs = lax.scan(advance, state_in, pieces)  48.8 us
    all_gather x1, waiting for transfers between devices, shards(): lax.all_gather(c_in, 'head', axis=0, tiled=True)  48 us
    another operation x91, other arithmetic  43.5 us
    dynamic_slice x40, local copies, waits for them, and re-layouts, shards(): sums, per_head = lax.scan(head_step, start, inputs)  43.1 us
    another operation x16, loops' own time, head_forward(): state_out, outputs = lax.scan(advance, state_in, pieces)  30.4 us
  transfers between devices with their start and end apart: 13, of which 11 were waited for; matrix products, arithmetic and copies ran while one was open for 6% of the time, Pallas kernels for 0%

commit v1 on v0

--- a/solution.py
+++ b/solution.py
@@ -9,6 +9,18 @@
 GROUPS = 8
 CONV = 4
 HIGH = lax.Precision.HIGHEST
+
+
+def feed_clusters(z, peer_axis, d0=0):
+    return jnp.concatenate(
+        lax.all_to_all(
+            jnp.stack([z for _ in range(lax.axis_size(peer_axis))], axis=0),
+            axis_name=peer_axis,
+            split_axis=0,
+            concat_axis=0,
+        ),
+        d0,
+    )
 
 
 def passed_along(value, axis, by):
@@ -98,10 +110,7 @@
         lax.all_to_all(grad_y, "head", split_axis=1, concat_axis=0, tiled=True),
         lax.all_to_all(dt, "head", split_axis=1, concat_axis=0, tiled=True),
     )
-    b_all, c_all = (
-        lax.all_gather(b_in, "head", axis=0, tiled=True),
-        lax.all_gather(c_in, "head", axis=0, tiled=True),
-    )
+    b_all, c_all = (lax.all_gather(b_in, "head", axis=0, tiled=True), feed_clusters(c_in, "head"))
     first = lax.axis_index("head") // per_group * STATE
     b_rows = lax.dynamic_slice_in_dim(b_all, first, STATE, 1)
     c_rows = lax.dynamic_slice_in_dim(c_all, first, STATE, 1)

time: 941 us -> 910 us (0.967)
  waiting for transfers between devices: 216 us -> 150 us
  blocking collectives: 22.8 us -> 55.5 us
    all_gather x1 -> x0, waiting for transfers between devices: 48 us -> none  [shards(): lax.all_gather(c_in, 'head', axis=0, tiled=True)]
    all_to_all x0 -> x2, blocking collectives: none -> 32.7 us  [the longest x1 19.2 us: shards(): lax.all_to_all(dt, 'head', split_axis=1, concat_axis=0, tiled=True)]
    all_gather x1, waiting for transfers between devices: 53.1 us -> 35.1 us  [shards(): lax.all_gather(b_in, 'head', axis=0, tiled=True)]
  transfers between devices with their start and end apart: 13 -> 11, of which waited for: 11 -> 9; matrix products, arithmetic and copies ran while one was open for 6% -> 6% of each run, Pallas kernels for 0% -> 0%
where the time goes in v1:
time: 910 us; the launch traced here: 901 us
  other arithmetic  272 us (30%)
  local copies, waits for them, and re-layouts  242 us (27%)
  waiting for transfers between devices  150 us (16%)
  matrix products  74.7 us (8%)
  blocking collectives  55.5 us (6%)
  starting transfers between devices  54.9 us (6%)
  loops' own time  36.3 us (4%)
  between operations  14.1 us (2%)
    all_gather x2, waiting for transfers between devices, entering(): everything = jax.tree.map(lambda part: lax.all_gather(part, axis), value)  61.8 us
    select_n x32, other arithmetic, hop(): return jax.tree.map(lambda a, b: jnp.where(reached, a, b), new, before)  52.8 us
    dynamic_update_slice x112, local copies, waits for them, and re-layouts, head_forward(): state_out, outputs = lax.scan(advance, state_in, pieces)  48.3 us
    another operation x91, other arithmetic  44 us
    dynamic_slice x40, local copies, waits for them, and re-layouts, shards(): sums, per_head = lax.scan(head_step, start, inputs)  43 us
    all_gather x1, waiting for transfers between devices, shards(): lax.all_gather(b_in, 'head', axis=0, tiled=True)  35.1 us
    another operation x16, loops' own time, head_forward(): state_out, outputs = lax.scan(advance, state_in, pieces)  33.4 us
    reduce_sum x16, other arithmetic, advance(): tail_wt = jnp.exp(cumul[-1] - cumul) * dt_part  30 us
  transfers between devices with their start and end apart: 11, of which 9 were waited for; matrix products, arithmetic and copies ran while one was open for 6% of the time, Pallas kernels for 0%

profile of v1, /device:TPU:1, one launch (start us, length us, event | category | flops | bytes accessed | tf_op | source)
XLA Modules:
  0.0 900.5 jit_solution(5044417318300034900)
XLA Ops:
  8.0 19.2 %all_to_all.120 = bf16[8,32,8]{2,0,1:T(8,128)(2,1)S(1)} all-to-all(bf16[8,32,8]{2,0,1:T(8,128)(2,1)S(1)} %copy.117), channel_id=1, replica_groups=mesh['ctx'=16,'head'=32] {'head'}, dimensions={1} | all-to-all | bytes 8192 | tf_op jit(solution)/shard_map/all_to_all | solution.py:111
  27.2 13.5 %all_to_all.121 = bf16[8,32,512]{2,0,1:T(8,128)(2,1)S(1)} all-to-all(bf16[8,32,512]{2,0,1:T(8,128)(2,1)} %bitcast.522), channel_id=1, replica_groups=mesh['ctx'=16,'head'=32] {'head'}, dimensions={1} | all-to-all | bytes 524288 | tf_op jit(solution)/shard_map/all_to_all | solution.py:110
  42.6 5.1 all-to-all-start.2
  53.8 16.6 %all-to-all-done.2 = bf16[32,8,2048]{2,1,0:T(8,128)(2,1)S(1)} async-done(((bf16[32,8,2048]{2,1,0:T(8,128)(2,1)}), bf16[32,8,2048]{2,1,0:T(8,128)(2,1)S(1)}, u32[]{:S(2)}, u32[]{:S(2)}) %all-to-all-start.2) | async-done | bytes 1048608 | tf_op jit(solution)/shard_map/all_to_all | solution.py:16
  72.3 8.0 all-to-all-start.3
  80.6 9.4 %all-to-all-done.3 = bf16[8,32,512]{2,0,1:T(8,128)(2,1)S(1)} async-done(((bf16[8,32,512]{2,0,1:T(8,128)(2,1)}), bf16[8,32,512]{2,0,1:T(8,128)(2,1)S(1)}, u32[]{:S(2)}, u32[]{:S(2)}) %all-to-all-start.3) | async-done | bytes 262176 | tf_op jit(solution)/shard_map/all_to_all | solution.py:109
  89.9 9.1 %collective-permute-start = (bf16[3,512]{1,0:T(4,128)(2,1)S(1)}, bf16[3,512]{1,0:T(4,128)(2,1)S(1)}, u32[]{:S(2)}, u32[]{:S(2)}) collective-permute-start(bf16[3,512]{1,0:T(4,128)(2,1)S(1)} %slice.212), channel_id=1, source_target_pairs={{0,32},{32,64},{64,96},{96,128},{128,160},{160,192},{192,224},{224... | collective-permute-start | bytes 9224 | tf_op jit(solution)/shard_map/ppermute | solution.py:29
  100.5 35.1 %all-gather.7.cloned.1.call-done = bf16[256,2048]{1,0:T(8,128)(2,1)} async-done(((bf16[8,2048]{1,0:T(8,128)(2,1)}), bf16[256,2048]{1,0:T(8,128)(2,1)}) %all-gather.7.cloned.1.call-update) | async-done | bytes 1048592 | tf_op jit(solution)/shard_map/all_gather | solution.py:113
  139.2 22.8 %all-gather.2 = f32[16,1,8]{2,1,0:T(1,128)S(1)} all-gather(f32[1,1,8]{2,1,0:T(1,128)S(1)} %bitcast.535), channel_id=1, replica_groups=mesh['ctx'=16,'head'=32] {'ctx'}, dimensions={0}, use_global_device_ids=true | all-gather | bytes 544 | tf_op jit(solution)/shard_map/all_gather | solution.py:34
  163.6 36.4 %all-gather.9.cloned.1.call-done = f32[128,64,256]{2,1,0:T(8,128)} async-done(((f32[8,64,256]{2,1,0:T(8,128)}), f32[128,64,256]{2,1,0:T(8,128)}) %all-gather.9.cloned.1.call-update) | async-done | bytes 8388624 | tf_op jit(solution)/shard_map/all_gather | solution.py:34
  199.9 34.1 %while.180 = (s32[]{:T(128)}, f32[8,64,256]{2,1,0:T(8,128)}, s32[]{:T(128)}, f32[16,8,64,256]{3,2,1,0:T(8,128)}, f32[16,8]{1,0:T(8,128)S(1)}, /*index=5*/s32[]{:T(128)}, s32[]{:T(128)}, s32[]{:T(128)}, s32[]{:T(128)}) while((s32[]{:T(128)}, f32[8,64,256]{2,1,0:T(8,128)}, s32[]{:T(128)}, f32[16,8,64,256]{3,2,1,0:T(8,128)}, ...), condition=%wide.region_5.6_spmd.clone, body=%wide.region_4.5_spmd.clone.sunk | while | flops 524296 | bytes 1573127 | solution.py:47
  199.9 2.0 fusion.141
  201.9 2.1 fusion.141
  204.1 2.1 fusion.141
  206.2 2.1 fusion.141
  208.3 2.1 fusion.141
  210.4 2.1 fusion.141
  212.6 2.1 fusion.141
  214.7 2.1 fusion.141
  216.8 2.1 fusion.141
  219.0 2.1 fusion.141
  221.1 2.2 fusion.141
  223.3 2.1 fusion.141
  225.4 2.2 fusion.141
  227.6 2.1 fusion.141
  229.8 2.2 fusion.141
  231.9 2.1 fusion.141
  234.1 25.4 %all-gather.11.cloned.1.call-done = f32[128,64,256]{2,1,0:T(8,128)} async-done(((f32[8,64,256]{2,1,0:T(8,128)}), f32[128,64,256]{2,1,0:T(8,128)}) %all-gather.11.cloned.1.call-update) | async-done | bytes 8388624 | tf_op jit(solution)/shard_map/all_gather | solution.py:34
  259.5 19.4 %while.181 = (s32[]{:T(128)}, f32[8,64,256]{2,1,0:T(8,128)S(1)}, s32[]{:T(128)}, f32[16,8]{1,0:T(8,128)S(1)}, f32[16,8,64,256]{3,2,1,0:T(8,128)}, /*index=5*/s32[]{:T(128)}, s32[]{:T(128)}) while((s32[]{:T(128)}, f32[8,64,256]{2,1,0:T(8,128)S(1)}, s32[]{:T(128)}, f32[16,8]{1,0:T(8,128)S(1)}, f32[16,8,64,256]{3,2,1,0:T(8,128)}, ...), condition=%wide.region_3.4_spmd.clone, body=%wide.region_2.3_spmd.clone.sunk | while | flops 524292 | bytes 1573065 | solution.py:47
  278.9 541.8 %while.184 = (s32[]{:T(128)}, f32[2,128,128]{2,1,0:T(8,128)}, f32[256,256]{1,0:T(8,128)}, f32[256,256]{1,0:T(8,128)}, f32[8,259,64]{1,2,0:T(8,128)}, /*index=5*/...) while((s32[]{:T(128)}, f32[2,128,128]{2,1,0:T(8,128)}, ...), condition=%wide.region_20.21_spmd.clone, body=%wide.region_6.20_spmd.clone.sunk | while | flops 177621440 | bytes 10403926 | solution.py:186
  279.6 3.0 constant_dynamic-slice_fusion.26
  286.6 12.2 %while.185 = (s32[]{:T(128)}, f32[64,256]{1,0:T(8,128)S(1)}, f32[2,128,128]{2,1,0:T(8,128)S(1)}, f32[2,128,128]{2,1,0:T(8,128)S(1)}, f32[2,1,128]{2,1,0:T(1,128)...) while((s32[]{:T(128)}, f32[64,256]{1,0:T(8,128)S(1)}, ...), condition=%wide.region_9.9_spmd.clone.clone, body=%wide.region_7.8_spmd.clone.clone.sunk | while | flops 50496128 | bytes 1198381 | solution.py:90
  303.0 33.7 %while.186 = (s32[]{:T(128)}, f32[64,256]{1,0:T(8,128)S(1)}, f32[2,128,64]{1,2,0:T(8,128)}, f32[2,128]{1,0:T(2,128)}, f32[2,128,128]{2,1,0:T(8,128)}, /*index=5*...) while((s32[]{:T(128)}, f32[64,256]{1,0:T(8,128)S(1)}, ...), condition=%wide.region_19.19_spmd.clone.clone, body=%wide.region_10.18_spmd.clone.clone.sunk | while | flops 126174464 | bytes 2319733 | solution.py:90
  346.4 3.0 constant_dynamic-slice_fusion.26
  353.4 12.2 %while.185 = (s32[]{:T(128)}, f32[64,256]{1,0:T(8,128)S(1)}, f32[2,128,128]{2,1,0:T(8,128)S(1)}, f32[2,128,128]{2,1,0:T(8,128)S(1)}, f32[2,1,128]{2,1,0:T(1,128)...) while((s32[]{:T(128)}, f32[64,256]{1,0:T(8,128)S(1)}, ...), condition=%wide.region_9.9_spmd.clone.clone, body=%wide.region_7.8_spmd.clone.clone.sunk | while | flops 50496128 | bytes 1198381 | solution.py:90
  369.8 33.7 %while.186 = (s32[]{:T(128)}, f32[64,256]{1,0:T(8,128)S(1)}, f32[2,128,64]{1,2,0:T(8,128)}, f32[2,128]{1,0:T(2,128)}, f32[2,128,128]{2,1,0:T(8,128)}, /*index=5*...) while((s32[]{:T(128)}, f32[64,256]{1,0:T(8,128)S(1)}, ...), condition=%wide.region_19.19_spmd.clone.clone, body=%wide.region_10.18_spmd.clone.clone.sunk | while | flops 126174464 | bytes 2319733 | solution.py:90
  408.7 1.9 bitcast_add_fusion.10
  414.3 3.0 constant_dynamic-slice_fusion.26
  421.3 12.2 %while.185 = (s32[]{:T(128)}, f32[64,256]{1,0:T(8,128)S(1)}, f32[2,128,128]{2,1,0:T(8,128)S(1)}, f32[2,128,128]{2,1,0:T(8,128)S(1)}, f32[2,1,128]{2,1,0:T(1,128)...) while((s32[]{:T(128)}, f32[64,256]{1,0:T(8,128)S(1)}, ...), condition=%wide.region_9.9_spmd.clone.clone, body=%wide.region_7.8_spmd.clone.clone.sunk | while | flops 50496128 | bytes 1198381 | solution.py:90
  437.6 33.7 %while.186 = (s32[]{:T(128)}, f32[64,256]{1,0:T(8,128)S(1)}, f32[2,128,64]{1,2,0:T(8,128)}, f32[2,128]{1,0:T(2,128)}, f32[2,128,128]{2,1,0:T(8,128)}, /*index=5*...) while((s32[]{:T(128)}, f32[64,256]{1,0:T(8,128)S(1)}, ...), condition=%wide.region_19.19_spmd.clone.clone, body=%wide.region_10.18_spmd.clone.clone.sunk | while | flops 126174464 | bytes 2319733 | solution.py:90
  482.2 3.0 constant_dynamic-slice_fusion.26
  489.1 12.2 %while.185 = (s32[]{:T(128)}, f32[64,256]{1,0:T(8,128)S(1)}, f32[2,128,128]{2,1,0:T(8,128)S(1)}, f32[2,128,128]{2,1,0:T(8,128)S(1)}, f32[2,1,128]{2,1,0:T(1,128)...) while((s32[]{:T(128)}, f32[64,256]{1,0:T(8,128)S(1)}, ...), condition=%wide.region_9.9_spmd.clone.clone, body=%wide.region_7.8_spmd.clone.clone.sunk | while | flops 50496128 | bytes 1198381 | solution.py:90
  505.5 33.7 %while.186 = (s32[]{:T(128)}, f32[64,256]{1,0:T(8,128)S(1)}, f32[2,128,64]{1,2,0:T(8,128)}, f32[2,128]{1,0:T(2,128)}, f32[2,128,128]{2,1,0:T(8,128)}, /*index=5*...) while((s32[]{:T(128)}, f32[64,256]{1,0:T(8,128)S(1)}, ...), condition=%wide.region_19.19_spmd.clone.clone, body=%wide.region_10.18_spmd.clone.clone.sunk | while | flops 126174464 | bytes 2319733 | solution.py:90
  550.0 3.0 constant_dynamic-slice_fusion.26
  557.0 12.2 %while.185 = (s32[]{:T(128)}, f32[64,256]{1,0:T(8,128)S(1)}, f32[2,128,128]{2,1,0:T(8,128)S(1)}, f32[2,128,128]{2,1,0:T(8,128)S(1)}, f32[2,1,128]{2,1,0:T(1,128)...) while((s32[]{:T(128)}, f32[64,256]{1,0:T(8,128)S(1)}, ...), condition=%wide.region_9.9_spmd.clone.clone, body=%wide.region_7.8_spmd.clone.clone.sunk | while | flops 50496128 | bytes 1198381 | solution.py:90
  573.4 33.7 %while.186 = (s32[]{:T(128)}, f32[64,256]{1,0:T(8,128)S(1)}, f32[2,128,64]{1,2,0:T(8,128)}, f32[2,128]{1,0:T(2,128)}, f32[2,128,128]{2,1,0:T(8,128)}, /*index=5*...) while((s32[]{:T(128)}, f32[64,256]{1,0:T(8,128)S(1)}, ...), condition=%wide.region_19.19_spmd.clone.clone, body=%wide.region_10.18_spmd.clone.clone.sunk | while | flops 126174464 | bytes 2319733 | solution.py:90
  617.9 3.0 constant_dynamic-slice_fusion.26
  624.8 12.2 %while.185 = (s32[]{:T(128)}, f32[64,256]{1,0:T(8,128)S(1)}, f32[2,128,128]{2,1,0:T(8,128)S(1)}, f32[2,128,128]{2,1,0:T(8,128)S(1)}, f32[2,1,128]{2,1,0:T(1,128)...) while((s32[]{:T(128)}, f32[64,256]{1,0:T(8,128)S(1)}, ...), condition=%wide.region_9.9_spmd.clone.clone, body=%wide.region_7.8_spmd.clone.clone.sunk | while | flops 50496128 | bytes 1198381 | solution.py:90
  641.2 33.7 %while.186 = (s32[]{:T(128)}, f32[64,256]{1,0:T(8,128)S(1)}, f32[2,128,64]{1,2,0:T(8,128)}, f32[2,128]{1,0:T(2,128)}, f32[2,128,128]{2,1,0:T(8,128)}, /*index=5*...) while((s32[]{:T(128)}, f32[64,256]{1,0:T(8,128)S(1)}, ...), condition=%wide.region_19.19_spmd.clone.clone, body=%wide.region_10.18_spmd.clone.clone.sunk | while | flops 126174464 | bytes 2319733 | solution.py:90
  685.7 3.0 constant_dynamic-slice_fusion.26
  692.7 12.2 %while.185 = (s32[]{:T(128)}, f32[64,256]{1,0:T(8,128)S(1)}, f32[2,128,128]{2,1,0:T(8,128)S(1)}, f32[2,128,128]{2,1,0:T(8,128)S(1)}, f32[2,1,128]{2,1,0:T(1,128)...) while((s32[]{:T(128)}, f32[64,256]{1,0:T(8,128)S(1)}, ...), condition=%wide.region_9.9_spmd.clone.clone, body=%wide.region_7.8_spmd.clone.clone.sunk | while | flops 50496128 | bytes 1198381 | solution.py:90
  709.1 33.7 %while.186 = (s32[]{:T(128)}, f32[64,256]{1,0:T(8,128)S(1)}, f32[2,128,64]{1,2,0:T(8,128)}, f32[2,128]{1,0:T(2,128)}, f32[2,128,128]{2,1,0:T(8,128)}, /*index=5*...) while((s32[]{:T(128)}, f32[64,256]{1,0:T(8,128)S(1)}, ...), condition=%wide.region_19.19_spmd.clone.clone, body=%wide.region_10.18_spmd.clone.clone.sunk | while | flops 126174464 | bytes 2319733 | solution.py:90
  753.6 3.0 constant_dynamic-slice_fusion.26
  760.6 12.2 %while.185 = (s32[]{:T(128)}, f32[64,256]{1,0:T(8,128)S(1)}, f32[2,128,128]{2,1,0:T(8,128)S(1)}, f32[2,128,128]{2,1,0:T(8,128)S(1)}, f32[2,1,128]{2,1,0:T(1,128)...) while((s32[]{:T(128)}, f32[64,256]{1,0:T(8,128)S(1)}, ...), condition=%wide.region_9.9_spmd.clone.clone, body=%wide.region_7.8_spmd.clone.clone.sunk | while | flops 50496128 | bytes 1198381 | solution.py:90
  777.0 33.7 %while.186 = (s32[]{:T(128)}, f32[64,256]{1,0:T(8,128)S(1)}, f32[2,128,64]{1,2,0:T(8,128)}, f32[2,128]{1,0:T(2,128)}, f32[2,128,128]{2,1,0:T(8,128)}, /*index=5*...) while((s32[]{:T(128)}, f32[64,256]{1,0:T(8,128)S(1)}, ...), condition=%wide.region_19.19_spmd.clone.clone, body=%wide.region_10.18_spmd.clone.clone.sunk | while | flops 126174464 | bytes 2319733 | solution.py:90
  823.5 9.3 %all-to-all-start.7 = ((f32[32,8,8]{1,2,0:T(8,128)}), f32[32,8,8]{1,2,0:T(8,128)S(1)}, u32[]{:S(2)}, u32[]{:S(2)}) async-start(f32[32,8,8]{1,2,0:T(8,128)} %copy.135), calls=%async_computation.7 | async-start | bytes 262144 | tf_op jit(solution)/shard_map/all_to_all | solution.py:199
  834.4 7.5 all-to-all-done.7
  841.9 4.4 all-to-all-start.6
  849.3 6.7 all-to-all-done.6
  856.0 6.3 all-to-all-start.5
  863.3 3.8 collective-permute-start.1
  868.4 2.9 collective-permute-done.1
  873.0 8.9 all-to-all-start.4
  883.9 9.4 %all-to-all-done.4 = bf16[32,8,512]{2,1,0:T(8,128)(2,1)S(1)} async-done(((bf16[32,8,512]{2,1,0:T(8,128)(2,1)}), bf16[32,8,512]{2,1,0:T(8,128)(2,1)S(1)}, u32[]{:S(2)}, u32[]{:S(2)}) %all-to-all-start.4) | async-done | bytes 262176 | tf_op jit(solution)/shard_map/all_to_all | solution.py:195
  (1205 shorter events, 530.3 us)
Async XLA Ops:
  7.2 73.2 %copy-start.11 = (f32[4,512]{1,0:T(4,128)S(1)}, f32[4,512]{1,0:T(4,128)}, u32[]{:S(2)}) copy-start(f32[4,512]{1,0:T(4,128)} %param.26) | copy-start | bytes 24580
  7.2 92.8 %copy-start.12 = (f32[512]{0:T(512)S(1)}, f32[512]{0:T(512)}, u32[]{:S(2)}) copy-start(f32[512]{0:T(512)} %param.27) | copy-start | bytes 6148
  42.6 27.8 %all-to-all-start.2 = ((bf16[32,8,2048]{2,1,0:T(8,128)(2,1)}), bf16[32,8,2048]{2,1,0:T(8,128)(2,1)S(1)}, u32[]{:S(2)}, u32[]{:S(2)}) async-start(bf16[32,8,2048]{2,1,0:T(8,128)(2,1)} %stack.2), calls=%async_computation.2 | async-start | bytes 2097152 | tf_op jit(solution)/shard_map/all_to_all | solution.py:16
  47.7 88.0 %all-gather.7.cloned.1.call-start = ((), (), s32[]{:S(2)}) async-start(), calls=%async_computation.8 | async-start | bytes 1081344 | tf_op jit(solution)/shard_map/all_gather | solution.py:113
  48.4 151.5 %all-gather.9.cloned.1.call-start = ((), (), s32[]{:S(2)}) async-start(), calls=%async_computation.9 | async-start | bytes 8912896 | tf_op jit(solution)/shard_map/all_gather | solution.py:34
  70.5 129.5 %copy-start.2 = (bf16[256,256]{1,0:T(8,128)(2,1)}, bf16[256,256]{1,0:T(8,128)(2,1)S(1)}, u32[]{:S(2)}) copy-start(bf16[256,256]{1,0:T(8,128)(2,1)S(1)} %get-tuple-element.2368) | copy-start | bytes 393220
  72.3 17.6 %all-to-all-start.3 = ((bf16[8,32,512]{2,0,1:T(8,128)(2,1)}), bf16[8,32,512]{2,0,1:T(8,128)(2,1)S(1)}, u32[]{:S(2)}, u32[]{:S(2)}) async-start(bf16[8,32,512]{2,0,1:T(8,128)(2,1)} %bitcast.523), calls=%async_computation.3 | async-start | bytes 524288 | tf_op jit(solution)/shard_map/all_to_all | solution.py:109
  80.3 179.2 %all-gather.11.cloned.1.call-start = ((), (), s32[]{:S(2)}) async-start(), calls=%async_computation.10 | async-start | bytes 8912896 | tf_op jit(solution)/shard_map/all_gather | solution.py:34
  89.9 9.9 %collective-permute-start = (bf16[3,512]{1,0:T(4,128)(2,1)S(1)}, bf16[3,512]{1,0:T(4,128)(2,1)S(1)}, u32[]{:S(2)}, u32[]{:S(2)}) collective-permute-start(bf16[3,512]{1,0:T(4,128)(2,1)S(1)} %slice.212), channel_id=1, source_target_pairs={{0,32},{32,64},{64,96},{96,128},{128,160},{160,192},{192,224},{224... | collective-permute-start | bytes 9224 | tf_op jit(solution)/shard_map/ppermute | solution.py:29
  136.6 122.9 %copy-start.1 = (bf16[256,256]{1,0:T(8,128)(2,1)}, bf16[256,256]{1,0:T(8,128)(2,1)S(1)}, u32[]{:S(2)}) copy-start(bf16[256,256]{1,0:T(8,128)(2,1)S(1)} %get-tuple-element.2370) | copy-start | bytes 393220
  279.6 6.3 copy-start.3
  279.6 6.3 copy-start.4
  279.6 6.3 copy-start.5
  279.6 6.3 copy-start.9
  298.9 2.2 copy-start.7
  298.9 2.2 copy-start.8
  298.9 2.2 copy-start.13
  346.4 6.3 copy-start.3
  346.4 6.3 copy-start.4
  346.4 6.3 copy-start.5
  346.4 6.3 copy-start.9
  365.6 2.2 copy-start.8
  365.6 2.2 copy-start.13
  414.3 6.3 copy-start.3
  414.3 6.3 copy-start.4
  414.3 6.3 copy-start.5
  414.3 6.3 copy-start.9
  433.5 2.2 copy-start.8
  433.5 2.2 copy-start.13
  482.1 6.3 copy-start.3
  482.1 6.3 copy-start.4
  482.1 6.3 copy-start.5
  482.1 6.3 copy-start.9
  501.4 2.2 copy-start.8
  501.4 2.2 copy-start.13
  550.0 6.3 copy-start.3
  550.0 6.3 copy-start.4
  550.0 6.3 copy-start.5
  550.0 6.3 copy-start.9
  569.2 2.2 copy-start.8
  569.2 2.2 copy-start.13
  617.8 6.3 copy-start.3
  617.8 6.3 copy-start.4
  617.9 6.3 copy-start.5
  617.9 6.3 copy-start.9
  637.1 2.2 copy-start.8
  637.1 2.2 copy-start.13
  685.7 6.3 copy-start.3
  685.7 6.3 copy-start.4
  685.7 6.3 copy-start.5
  685.7 6.3 copy-start.9
  705.0 2.2 copy-start.8
  705.0 2.2 copy-start.13
  753.6 6.3 copy-start.3
  753.6 6.3 copy-start.4
  753.6 6.3 copy-start.5
  753.6 6.3 copy-start.9
  772.8 2.2 copy-start.8
  772.8 2.2 copy-start.13
  823.5 18.4 %all-to-all-start.7 = ((f32[32,8,8]{1,2,0:T(8,128)}), f32[32,8,8]{1,2,0:T(8,128)S(1)}, u32[]{:S(2)}, u32[]{:S(2)}) async-start(f32[32,8,8]{1,2,0:T(8,128)} %copy.135), calls=%async_computation.7 | async-start | bytes 262144 | tf_op jit(solution)/shard_map/all_to_all | solution.py:199
  841.9 14.1 %all-to-all-start.6 = ((f32[32,8,256]{2,1,0:T(8,128)}), f32[32,8,256]{2,1,0:T(8,128)S(1)}, u32[]{:S(2)}, u32[]{:S(2)}) async-start(f32[32,8,256]{2,1,0:T(8,128)} %bitcast.45), calls=%async_computation.6 | async-start | bytes 524288 | tf_op jit(solution)/shard_map/all_to_all | solution.py:201
  856.0 17.0 %all-to-all-start.5 = ((f32[32,8,256]{2,1,0:T(8,128)}), f32[32,8,256]{2,1,0:T(8,128)S(1)}, u32[]{:S(2)}, u32[]{:S(2)}) async-start(f32[32,8,256]{2,1,0:T(8,128)} %bitcast.40), calls=%async_computation.5 | async-start | bytes 524288 | tf_op jit(solution)/shard_map/all_to_all | solution.py:200
  863.3 8.0 collective-permute-start.1
  873.0 20.3 %all-to-all-start.4 = ((bf16[32,8,512]{2,1,0:T(8,128)(2,1)}), bf16[32,8,512]{2,1,0:T(8,128)(2,1)S(1)}, u32[]{:S(2)}, u32[]{:S(2)}) async-start(bf16[32,8,512]{2,1,0:T(8,128)(2,1)} %bitcast.36), calls=%async_computation.4 | async-start | bytes 524288 | tf_op jit(solution)/shard_map/all_to_all | solution.py:195
  (31 other events, 68.5 us)
Sparse Core Ops, SparseCore 0:
  51.7 83.8 all-gather.6
  137.7 62.1 all-gather.8
  202.1 57.3 all-gather.10
